TPU v7x, 256 devices: a whole 4x4x8 slice. The times are simulated.
256 devices in a mesh: gz: 8 (over y, core), gx: 8 (over x, z_lo), gy: 4 (over z_hi).
Axes of the slice: x: 4, y: 4, z: 8 (z_hi: 4, z_lo: 2; z = z_hi * 2 + z_lo), core: 2. Of those that a mesh axis runs over, the one named last changes fastest.
Arguments:
- initial_field: float32 [16, 1024, 512], P('gz', 'gx', 'gy'), may hold values from -6 to 6
- source_term: float32 [16, 1024, 512], P('gz', 'gx', 'gy'), may hold values from -48 to 48
- block_inverse: float32 [1024, 512, 128], P('gx', 'gy'), may hold values from -0.1 to 0.1
Outputs:
- smoothed: float32 [16, 1024, 512], P('gz', 'gx', 'gy')
All inputs are finite; a program needn't handle non-finite values.
Results may differ from a plain program's by a relative error of at most 0.00013.
Values sent between devices are 32-bit elements; how exact they have to be, the bound alone decides.
A program may use at most 64 MiB of HBM per device.

v0:
```python
import jax
import jax.numpy as jnp
from jax import lax
from jax.sharding import PartitionSpec as P

exact_mode = lax.Precision.HIGHEST


def extended_2(cells, sides, width):
    for axis, dim in sides:
        count = lax.axis_size(axis)
        ends = count - 1
        head = lax.slice_in_dim(cells, 0, width, axis=dim)
        tail = lax.slice_in_dim(cells, cells.shape[dim] - width, cells.shape[dim], axis=dim)
        cells = jnp.concatenate(
            [
                lax.ppermute(tail, axis, [(i, (i + 1) % count) for i in range(ends)]),
                cells,
                lax.ppermute(head, axis, [((i + 1) % count, i) for i in range(ends)]),
            ],
            axis=dim,
        )
    return cells


def passed_along(value, axis, steps):
    count = lax.axis_size(axis)
    first, last = (max(0, -steps), min(count, count - steps))
    return lax.ppermute(value, axis, [(source, source + steps) for source in range(first, last)])


def box_sum(extended):
    row_sums = extended[:-2] + extended[1:-1] + extended[2:]
    return row_sums[:, :-2] + row_sums[:, 1:-1] + row_sums[:, 2:]


def relax_plane(under_ext, current, over_ext, source_plane, inverse_rows):
    neighbours = box_sum(under_ext) + box_sum(current) + box_sum(over_ext)
    interior = current[1:-1, 1:-1]
    residual = source_plane - (27.0 * interior - neighbours)
    return interior + jnp.einsum("xij,xj->xi", inverse_rows, residual, precision=exact_mode)


def add_rim(plane):
    return extended_2(plane, (("gx", 0), ("gy", 1)), 1)


def run_chain(initial_field, source_term, block_inverse):
    planes_dev = initial_field.shape[0]
    chain_len = lax.axis_size("gz")
    position = lax.axis_index("gz")

    def relax_here(under_ext, current, over_ext, source_plane):
        return relax_plane(under_ext, current, over_ext, source_plane, block_inverse)

    def keep_plane(under_ext, current, over_ext, source_plane):
        return current[1:-1, 1:-1]

    old_ext = extended_2(initial_field, (("gx", 1), ("gy", 2)), 1)
    over_slab = passed_along(old_ext[0], "gz", -1)
    zero_ext = jnp.zeros_like(old_ext[0])

    def forward_section(section_num, state_now):
        fwd_ext, below_keep = state_now
        active = section_num == position
        incoming = passed_along(fwd_ext[planes_dev - 1, 1:-1, 1:-1], "gz", 1)
        under_ext = add_rim(incoming)
        below_keep = jnp.where(active, under_ext, below_keep)
        planes = []
        lower_ext = under_ext
        for j in range(planes_dev):
            upper_ext = fwd_ext[j + 1] if j + 1 < planes_dev else over_slab
            fresh = lax.cond(
                active, relax_here, keep_plane, lower_ext, fwd_ext[j], upper_ext, source_term[j]
            )
            fresh_ext = jnp.where(active, add_rim(fresh), fwd_ext[j])
            planes.append(fresh_ext)
            lower_ext = fresh_ext
        return (jnp.stack(planes), below_keep)

    fwd_ext, below_keep = lax.fori_loop(0, chain_len, forward_section, (old_ext, zero_ext))

    def backward_section(section_num, bwd_ext):
        active = section_num == chain_len - 1 - position
        incoming = passed_along(bwd_ext[0, 1:-1, 1:-1], "gz", -1)
        over_ext = add_rim(incoming)
        planes = [None] * planes_dev
        upper_ext = over_ext
        for j in reversed(range(planes_dev)):
            lower_ext = fwd_ext[j - 1] if j > 0 else below_keep
            fresh = lax.cond(
                active, relax_here, keep_plane, lower_ext, bwd_ext[j], upper_ext, source_term[j]
            )
            if j > 0:
                fresh_ext = jnp.where(active, add_rim(fresh), bwd_ext[j])
            else:
                fresh_ext = jnp.where(active, jnp.pad(fresh, 1), bwd_ext[j])
            planes[j] = fresh_ext
            upper_ext = fresh_ext
        return jnp.stack(planes)

    bwd_ext = lax.fori_loop(0, chain_len, backward_section, fwd_ext)
    return bwd_ext[:, 1:-1, 1:-1]


def body(initial_field, source_term, block_inverse):
    return run_chain(initial_field, source_term, block_inverse)


def solution(mesh):
    placed = (P("gz", "gx", "gy"), P("gz", "gx", "gy"), P("gx", "gy", None))
    return jax.shard_map(
        body, mesh=mesh, in_specs=placed, out_specs=P("gz", "gx", "gy"), check_vma=False
    )
```

profile of v0, /device:TPU:166, one launch (start us, length us, event | category | flops | bytes accessed | tf_op | source)
XLA Modules:
  0.0 1350.3 jit_solution(11736237281752747053)
XLA Ops:
  25.7 613.5 %while.32 = (s32[]{:T(128)}, f32[2,130,130]{2,1,0:T(8,128)S(1)}, f32[130,130]{1,0:T(8,128)S(1)}, s32[]{:T(128)}, f32[2,128,128]{2,1,0:T(8,128)}, /*index=5*/f32[...) while((s32[]{:T(128)}, f32[2,130,130]{2,1,0:T(8,128)S(1)}, ...), condition=%wide.region_5.6_spmd.clone, body=%wide.region_0.5_spmd.clone.sunk | while | flops 51345488 | bytes 23155080 | solution.py:81
  25.8 5.0 collective-permute-start.9
  41.4 5.5 collective-permute-start.12
  49.3 6.7 collective-permute-done.13
  56.1 16.6 %conditional.12 = (f32[128,128]{1,0:T(8,128)S(1)}) conditional(s32[]{:T(128)} %convert_element_type.31, f32[130,130]{1,0:T(8,128)S(1)} %get-tuple-element.664, (f32[130,130]{1,0:T(8,128)S(1)}, f32[2,128,128]{2,1,0:T(8,128)}, f32[130,130]{1,0:T(8,128)S(1)}, f32[130,130]{1,0:T(8,128)S(1)}, f32[128,128,128]{2,1,0:T(8,128)}) %tuple.176), branch_computations={%region_1.1_spmd, %region_2.2_spmd} | conditional | flops 25462272 | bytes 10301448 | solution.py:73
  57.3 15.4 %fusion.31 = f32[128,1,128]{2,1,0:T(1,128)S(1)} fusion(f32[128,128,1]{1,2,0:T(1,128)S(1)} %bitcast.104, f32[128,128,128]{2,1,0:T(8,128)} %get-tuple-element.392), kind=kOutput, calls=%fused_computation.98 | convolution fusion | flops 25165824 | bytes 8519680 | tf_op jit(solution)/shard_map/while/body/eval_jaxpr/cond/branch_1_fun/xij,xj->xi/dot_general | solution.py:41
  92.9 16.7 %conditional.13 = (f32[128,128]{1,0:T(8,128)S(1)}) conditional(s32[]{:T(128)} %convert_element_type.31, f32[130,130]{1,0:T(8,128)S(1)} %get-tuple-element.670, (f32[130,130]{1,0:T(8,128)S(1)}, f32[2,128,128]{2,1,0:T(8,128)}, pred[130,130]{1,0:T(8,128)(4,1)S(1)}, f32[130,130]{1,0:T(8,128)S(1)}, f32[130,130]{1,0:T(8,128)S(1)}, ...), branch_computations={%region_3.3_spmd, %region_4.4_spmd} | conditional | flops 25479172 | bytes 10521148 | solution.py:73
  94.1 15.4 %fusion.32 = f32[128,1,128]{2,1,0:T(1,128)S(1)} fusion(f32[128,128,1]{1,2,0:T(1,128)S(1)} %bitcast.105, f32[128,128,128]{2,1,0:T(8,128)} %get-tuple-element.399), kind=kOutput, calls=%fused_computation.99 | convolution fusion | flops 25165824 | bytes 8519680 | tf_op jit(solution)/shard_map/while/body/eval_jaxpr/cond/branch_1_fun/xij,xj->xi/dot_general | solution.py:41
  190.0 27.6 %collective-permute-start.9 = (f32[128,128]{1,0:T(8,128)S(1)}, f32[128,128]{1,0:T(8,128)S(1)}, u32[]{:S(2)}, u32[]{:S(2)}) collective-permute-start(f32[128,128]{1,0:T(8,128)S(1)} %slice_bitcast_fusion.16), channel_id=1, source_target_pairs={{0,32},{32,64},{64,96},{96,128},{128,160},{160,192},{192,224},{1,3... | collective-permute-start | bytes 196616 | tf_op jit(solution)/shard_map/while/body/eval_jaxpr/ppermute | solution.py:29
  229.9 4.8 collective-permute-start.13
  250.2 4.8 collective-permute-start.17
  339.1 31.1 %collective-permute-start.9 = (f32[128,128]{1,0:T(8,128)S(1)}, f32[128,128]{1,0:T(8,128)S(1)}, u32[]{:S(2)}, u32[]{:S(2)}) collective-permute-start(f32[128,128]{1,0:T(8,128)S(1)} %slice_bitcast_fusion.16), channel_id=1, source_target_pairs={{0,32},{32,64},{64,96},{96,128},{128,160},{160,192},{192,224},{1,3... | collective-permute-start | bytes 196616 | tf_op jit(solution)/shard_map/while/body/eval_jaxpr/ppermute | solution.py:29
  382.2 4.8 collective-permute-start.13
  420.7 4.8 collective-permute-start.21
  465.1 4.8 collective-permute-start.17
  484.7 4.8 collective-permute-start.21
  493.8 25.0 %collective-permute-start.9 = (f32[128,128]{1,0:T(8,128)S(1)}, f32[128,128]{1,0:T(8,128)S(1)}, u32[]{:S(2)}, u32[]{:S(2)}) collective-permute-start(f32[128,128]{1,0:T(8,128)S(1)} %slice_bitcast_fusion.16), channel_id=1, source_target_pairs={{0,32},{32,64},{64,96},{96,128},{128,160},{160,192},{192,224},{1,3... | collective-permute-start | bytes 196616 | tf_op jit(solution)/shard_map/while/body/eval_jaxpr/ppermute | solution.py:29
  639.3 710.3 %while.31 = (s32[]{:T(128)}, f32[2,130,130]{2,1,0:T(8,128)S(1)}, s32[]{:T(128)}, f32[2,128,128]{2,1,0:T(8,128)}, f32[2,130,130]{2,1,0:T(8,128)S(1)}, /*index=5*/...) while((s32[]{:T(128)}, f32[2,130,130]{2,1,0:T(8,128)S(1)}, s32[]{:T(128)}, ...), condition=%wide.region_11.12_spmd, body=%wide.region_6.11_spmd.sunk | while | flops 51244608 | bytes 22940776 | solution.py:102
  640.9 27.7 %collective-permute-done = f32[128,128]{1,0:T(8,128)S(1)} collective-permute-done((f32[128,128]{1,0:T(8,128)S(1)}, f32[128,128]{1,0:T(8,128)S(1)}, u32[]{:S(2)}, u32[]{:S(2)}) %collective-permute-start) | collective-permute-done | bytes 65568 | tf_op jit(solution)/shard_map/while/body/eval_jaxpr/ppermute | solution.py:29
  708.5 7.2 collective-permute-done
  756.3 24.4 %collective-permute-done = f32[128,128]{1,0:T(8,128)S(1)} collective-permute-done((f32[128,128]{1,0:T(8,128)S(1)}, f32[128,128]{1,0:T(8,128)S(1)}, u32[]{:S(2)}, u32[]{:S(2)}) %collective-permute-start) | collective-permute-done | bytes 65568 | tf_op jit(solution)/shard_map/while/body/eval_jaxpr/ppermute | solution.py:29
  790.7 4.8 collective-permute-start.4
  809.7 4.8 collective-permute-start.8
  820.7 7.0 collective-permute-done
  867.7 27.2 %collective-permute-done = f32[128,128]{1,0:T(8,128)S(1)} collective-permute-done((f32[128,128]{1,0:T(8,128)S(1)}, f32[128,128]{1,0:T(8,128)S(1)}, u32[]{:S(2)}, u32[]{:S(2)}) %collective-permute-start) | collective-permute-done | bytes 65568 | tf_op jit(solution)/shard_map/while/body/eval_jaxpr/ppermute | solution.py:29
  934.8 7.2 collective-permute-done
  982.7 24.1 %collective-permute-done = f32[128,128]{1,0:T(8,128)S(1)} collective-permute-done((f32[128,128]{1,0:T(8,128)S(1)}, f32[128,128]{1,0:T(8,128)S(1)}, u32[]{:S(2)}, u32[]{:S(2)}) %collective-permute-start) | collective-permute-done | bytes 65568 | tf_op jit(solution)/shard_map/while/body/eval_jaxpr/ppermute | solution.py:29
  1046.8 229.8 %collective-permute-done = f32[128,128]{1,0:T(8,128)S(1)} collective-permute-done((f32[128,128]{1,0:T(8,128)S(1)}, f32[128,128]{1,0:T(8,128)S(1)}, u32[]{:S(2)}, u32[]{:S(2)}) %collective-permute-start) | collective-permute-done | bytes 65568 | tf_op jit(solution)/shard_map/while/body/eval_jaxpr/ppermute | solution.py:29
  1295.3 16.6 %conditional.10 = (f32[128,128]{1,0:T(8,128)S(1)}) conditional(s32[]{:T(128)} %convert_element_type.30, f32[130,130]{1,0:T(8,128)S(1)} %slice_bitcast_fusion.12, (f32[130,130]{1,0:T(8,128)S(1)}, f32[2,128,128]{2,1,0:T(8,128)}, f32[2,130,130]{2,1,0:T(8,128)S(1)}, f32[130,130]{1,0:T(8,128)S(1)}, f32[128,128,128]{2,1,0:T(8,128)}) %tuple.162), branch_computations={%region_7.7_spmd, %region_8.8_spmd} | conditional | flops 25462272 | bytes 10301448 | solution.py:91
  1296.4 15.4 %fusion.33 = f32[128,1,128]{2,1,0:T(1,128)S(1)} fusion(f32[128,128,1]{1,2,0:T(1,128)S(1)} %bitcast.106, f32[128,128,128]{2,1,0:T(8,128)} %get-tuple-element.412), kind=kOutput, calls=%fused_computation.100 | convolution fusion | flops 25165824 | bytes 8519680 | tf_op jit(solution)/shard_map/while/body/eval_jaxpr/cond/branch_1_fun/xij,xj->xi/dot_general | solution.py:41
  1332.7 16.8 %conditional.11 = (f32[130,130]{1,0:T(8,128)S(1)}) conditional(s32[]{:T(128)} %convert_element_type.30, f32[130,130]{1,0:T(8,128)S(1)} %get-tuple-element.656, (f32[130,130]{1,0:T(8,128)S(1)}, f32[2,128,128]{2,1,0:T(8,128)}, f32[130,130]{1,0:T(8,128)S(1)}, pred[130,130]{1,0:T(8,128)(4,1)S(1)}, f32[130,130]{1,0:T(8,128)S(1)}, ...), branch_computations={%region_9.9_spmd, %region_10.10_spmd} | conditional | flops 25479172 | bytes 10654288 | solution.py:91
  1333.9 15.4 %fusion.34 = f32[128,1,128]{2,1,0:T(1,128)S(1)} fusion(f32[128,128,1]{1,2,0:T(1,128)S(1)} %bitcast.107, f32[128,128,128]{2,1,0:T(8,128)} %get-tuple-element.419), kind=kOutput, calls=%fused_computation.101 | convolution fusion | flops 25165824 | bytes 8519680 | tf_op jit(solution)/shard_map/while/body/eval_jaxpr/cond/branch_1_fun/xij,xj->xi/dot_general | solution.py:41
  (670 shorter events, 793.6 us)
Async XLA Ops:
  8.9 11.6 collective-permute-start.24
  12.3 9.1 collective-permute-start.25
  46.9 9.1 collective-permute-start.13
  190.0 28.5 %collective-permute-start.9 = (f32[128,128]{1,0:T(8,128)S(1)}, f32[128,128]{1,0:T(8,128)S(1)}, u32[]{:S(2)}, u32[]{:S(2)}) collective-permute-start(f32[128,128]{1,0:T(8,128)S(1)} %slice_bitcast_fusion.16), channel_id=1, source_target_pairs={{0,32},{32,64},{64,96},{96,128},{128,160},{160,192},{192,224},{1,3... | collective-permute-start | bytes 196616 | tf_op jit(solution)/shard_map/while/body/eval_jaxpr/ppermute | solution.py:29
  250.2 9.1 collective-permute-start.17
  339.1 32.0 %collective-permute-start.9 = (f32[128,128]{1,0:T(8,128)S(1)}, f32[128,128]{1,0:T(8,128)S(1)}, u32[]{:S(2)}, u32[]{:S(2)}) collective-permute-start(f32[128,128]{1,0:T(8,128)S(1)} %slice_bitcast_fusion.16), channel_id=1, source_target_pairs={{0,32},{32,64},{64,96},{96,128},{128,160},{160,192},{192,224},{1,3... | collective-permute-start | bytes 196616 | tf_op jit(solution)/shard_map/while/body/eval_jaxpr/ppermute | solution.py:29
  401.7 9.1 collective-permute-start.17
  420.7 9.1 collective-permute-start.21
  445.8 9.1 collective-permute-start.13
  465.1 9.1 collective-permute-start.17
  493.8 25.9 %collective-permute-start.9 = (f32[128,128]{1,0:T(8,128)S(1)}, f32[128,128]{1,0:T(8,128)S(1)}, u32[]{:S(2)}, u32[]{:S(2)}) collective-permute-start(f32[128,128]{1,0:T(8,128)S(1)} %slice_bitcast_fusion.16), channel_id=1, source_target_pairs={{0,32},{32,64},{64,96},{96,128},{128,160},{160,192},{192,224},{1,3... | collective-permute-start | bytes 196616 | tf_op jit(solution)/shard_map/while/body/eval_jaxpr/ppermute | solution.py:29
  529.6 9.1 collective-permute-start.13
  548.6 9.1 collective-permute-start.17
  591.9 9.1 collective-permute-start.13
  611.0 9.1 collective-permute-start.17
  630.0 9.1 collective-permute-start.21
  639.6 29.0 %collective-permute-start = (f32[128,128]{1,0:T(8,128)S(1)}, f32[128,128]{1,0:T(8,128)S(1)}, u32[]{:S(2)}, u32[]{:S(2)}) collective-permute-start(f32[128,128]{1,0:T(8,128)S(1)} %slice_bitcast_fusion.13), channel_id=1, source_target_pairs={{32,0},{64,32},{96,64},{128,96},{160,128},{192,160},{224,192},{33,... | collective-permute-start | bytes 196616 | tf_op jit(solution)/shard_map/while/body/eval_jaxpr/ppermute | solution.py:29
  678.5 9.1 collective-permute-start.4
  697.5 9.1 collective-permute-start.8
  726.3 9.1 collective-permute-start.4
  745.3 9.1 collective-permute-start.8
  755.0 25.7 %collective-permute-start = (f32[128,128]{1,0:T(8,128)S(1)}, f32[128,128]{1,0:T(8,128)S(1)}, u32[]{:S(2)}, u32[]{:S(2)}) collective-permute-start(f32[128,128]{1,0:T(8,128)S(1)} %slice_bitcast_fusion.13), channel_id=1, source_target_pairs={{32,0},{64,32},{96,64},{128,96},{160,128},{192,160},{224,192},{33,... | collective-permute-start | bytes 196616 | tf_op jit(solution)/shard_map/while/body/eval_jaxpr/ppermute | solution.py:29
  790.7 9.1 collective-permute-start.4
  809.7 9.1 collective-permute-start.8
  837.7 9.1 collective-permute-start.4
  866.4 28.5 %collective-permute-start = (f32[128,128]{1,0:T(8,128)S(1)}, f32[128,128]{1,0:T(8,128)S(1)}, u32[]{:S(2)}, u32[]{:S(2)}) collective-permute-start(f32[128,128]{1,0:T(8,128)S(1)} %slice_bitcast_fusion.13), channel_id=1, source_target_pairs={{32,0},{64,32},{96,64},{128,96},{160,128},{192,160},{224,192},{33,... | collective-permute-start | bytes 196616 | tf_op jit(solution)/shard_map/while/body/eval_jaxpr/ppermute | solution.py:29
  923.8 9.1 collective-permute-start.8
  971.7 9.1 collective-permute-start.8
  981.4 25.4 %collective-permute-start = (f32[128,128]{1,0:T(8,128)S(1)}, f32[128,128]{1,0:T(8,128)S(1)}, u32[]{:S(2)}, u32[]{:S(2)}) collective-permute-start(f32[128,128]{1,0:T(8,128)S(1)} %slice_bitcast_fusion.13), channel_id=1, source_target_pairs={{32,0},{64,32},{96,64},{128,96},{160,128},{192,160},{224,192},{33,... | collective-permute-start | bytes 196616 | tf_op jit(solution)/shard_map/while/body/eval_jaxpr/ppermute | solution.py:29
  1035.7 9.1 collective-permute-start.8
  1045.5 231.1 %collective-permute-start = (f32[128,128]{1,0:T(8,128)S(1)}, f32[128,128]{1,0:T(8,128)S(1)}, u32[]{:S(2)}, u32[]{:S(2)}) collective-permute-start(f32[128,128]{1,0:T(8,128)S(1)} %slice_bitcast_fusion.13), channel_id=1, source_target_pairs={{32,0},{64,32},{96,64},{128,96},{160,128},{192,160},{224,192},{33,... | collective-permute-start | bytes 196616 | tf_op jit(solution)/shard_map/while/body/eval_jaxpr/ppermute | solution.py:29
  1323.4 9.1 collective-permute-start.8
  (149 other events, 888.6 us)
where the time goes:
time: 1360 us; the launch traced here: 1350 us
  waiting for transfers between devices  700 us (51%)
  starting transfers between devices  560 us (41%)
  matrix products  61.5 us (5%)
  other arithmetic  14.5 us (1%)
    ppermute x17, waiting for transfers between devices, passed_along(): lax.ppermute(value, axis, [(source, source + steps) for source in range(f...  364 us
    ppermute x82, waiting for transfers between devices, extended_2(): lax.ppermute(tail, axis, [(i, (i + 1) % count) for i in range(ends)])  316 us
    ppermute x82, starting transfers between devices, extended_2(): lax.ppermute(tail, axis, [(i, (i + 1) % count) for i in range(ends)])  246 us
    ppermute x82, starting transfers between devices, extended_2(): lax.ppermute(head, axis, [((i + 1) % count, i) for i in range(ends)])  202 us
    ppermute x17, starting transfers between devices, passed_along(): lax.ppermute(value, axis, [(source, source + steps) for source in range(f...  112 us
    dot_general x4, matrix products, relax_plane(): jnp.einsum('xij,xj->xi', inverse_rows, residual, precision=exact_mode)  61.5 us
  transfers between devices with their start and end apart: 181, of which 140 were waited for; matrix products, arithmetic and copies ran while one was open for 0% of the time, Pallas kernels for 0%

commit v1 on v0

v1 whole, which is shorter than its diff:
```python
import jax
import jax.numpy as jnp
from jax import lax
from jax.experimental import pallas as pl
from jax.experimental.pallas import tpu as pltpu
from jax.sharding import PartitionSpec as P

MESH = pl.DeviceIdType.MESH
NZ = 16
OWN = 16
HALO = 8
WIN = OWN + 2 * HALO
GROUPS = 4
STEPS = 4
ROUNDS = 2 * NZ // STEPS
GZ, GX, GY = 8, 8, 4
TAPS = tuple((lag, off) for lag in (1, 2, 3) for off in range(1 - lag, lag))
TAP_ROWS = 40


def lane_roll(x, amount):
    return x if amount % 128 == 0 else pltpu.roll(x, amount % 128, axis=1)


def box_x(x):
    return x + lane_roll(x, 1) + lane_roll(x, -1)


def lane_group(shape):
    return lax.broadcasted_iota(jnp.int32, shape, 1) // WIN


def unpack(packed):
    group = lane_group(packed.shape)
    turned = [lane_roll(packed, WIN * m) for m in range(GROUPS)]
    parts = []
    for h in range(GROUPS):
        part = turned[3]
        for m in (2, 1, 0):
            part = jnp.where(group == (h + m) % GROUPS, turned[m], part)
        parts.append(part)
    return jnp.concatenate(parts, axis=0)


def pack(field):
    rows = field.shape[0] // GROUPS
    group = lane_group((rows, 128))
    out = field[3 * rows :]
    for h in (2, 1, 0):
        out = jnp.where(group == h, field[h * rows : (h + 1) * rows], out)
    return out


def row_sums(accs):
    sub = lax.broadcasted_iota(jnp.int32, (8, 128), 0)
    for dist in (4, 2, 1):
        low = (sub // dist) % 2 == 0
        accs = [
            jnp.where(
                low,
                accs[k] + pltpu.roll(accs[k], 8 - dist, axis=0),
                accs[k + dist] + pltpu.roll(accs[k + dist], dist, axis=0),
            )
            for k in range(dist)
        ]
    return accs[0]


def swap_edges(edges):
    row = lax.broadcasted_iota(jnp.int32, (8, 128), 0)
    swapped = jnp.where(row % 2 == 0, pltpu.roll(edges, 1, axis=0), pltpu.roll(edges, 7, axis=0))
    swapped = jnp.where((row == 0) | (row == 7), 0.0, swapped)
    return box_x(swapped)


def swap_sides(x):
    row = lax.broadcasted_iota(jnp.int32, (8, 128), 0)
    return jnp.where(row % 2 == 0, pltpu.roll(x, 7, axis=0), pltpu.roll(x, 1, axis=0))


def kernel(
    v_ref, s_ref, a_ref, o_ref,
    aw, a2, win_v, win_s, field, source, base, edge, prev, shift, inject,
    phi_out, phi_in, phi, ve_out, ve_in, g_out, g_in, taps, cols, rows_t,
    xs, xr, xs_last, xr_last, g_stage, out_buf,
    al_sem, ar_send, ar_recv, w_send, w_recv, wx_send, wx_recv,
    phi_send, phi_recv, ve_send, ve_recv, g_send, g_recv,
    x_send, x_recv, f_send, f_recv,
):
    iz, ix, iy = lax.axis_index("gz"), lax.axis_index("gx"), lax.axis_index("gy")
    even = 1 - ix % 2
    p = even * iz + (1 - even) * (7 - iz)
    first, last = 1 - (p + 7) // 8, p // 7
    sign = 2 * even - 1
    lz, lx = iz - sign * (1 - first), ix - first
    rz, rx = iz + sign * (1 - last), ix + last
    has_left, has_right = lx >= 0, rx < GX
    cross_left, cross_right = (p == 0) & (ix > 0), (p == 7) & (ix < GX - 1)
    next_first, prev_last = 7 * even, 7 * (1 - even)

    def dev(z, x, y):
        return {"gz": z, "gx": x, "gy": y}

    def remote(src, dst, send, recv, target):
        return pltpu.make_async_remote_copy(
            src_ref=src, dst_ref=dst, send_sem=send, recv_sem=recv, device_id=target, device_id_type=MESH
        )

    a_mid = pltpu.make_async_copy(a_ref.at[pl.ds(16 * p, 16)], aw.at[pl.ds(8, 16)], al_sem.at[0])
    a_mid.start()

    def a_low():
        return pltpu.make_async_copy(a_ref.at[pl.ds(16 * p - 8, 8)], aw.at[pl.ds(0, 8)], al_sem.at[1])

    def a_high():
        return pltpu.make_async_copy(a_ref.at[pl.ds(16 * p + 16, 8)], aw.at[pl.ds(24, 8)], al_sem.at[2])

    @pl.when(p > 0)
    def _():
        a_low().start()

    @pl.when(p < 7)
    def _():
        a_high().start()

    @pl.when(jnp.logical_not(has_left))
    def _():
        aw[0:8] = jnp.zeros((8, 128, 128), jnp.float32)
        win_v[:, 0:8] = jnp.zeros((NZ, 8, 128), jnp.float32)
        win_s[:, 0:8] = jnp.zeros((NZ, 8, 128), jnp.float32)
        xr[0] = jnp.zeros(xr.shape[1:], jnp.float32)
        xr_last[0] = jnp.zeros(xr_last.shape[1:], jnp.float32)

    @pl.when(jnp.logical_not(has_right))
    def _():
        aw[24:32] = jnp.zeros((8, 128, 128), jnp.float32)
        win_v[:, 24:32] = jnp.zeros((NZ, 8, 128), jnp.float32)
        win_s[:, 24:32] = jnp.zeros((NZ, 8, 128), jnp.float32)
        xr[1] = jnp.zeros(xr.shape[1:], jnp.float32)
        xr_last[1] = jnp.zeros(xr_last.shape[1:], jnp.float32)

    barrier = pltpu.get_barrier_semaphore()

    def greet(z, x, y):
        pl.semaphore_signal(barrier, inc=1, device_id=dev(z, x, y), device_id_type=MESH)

    for k in range(1, GZ):
        greet((iz + k) % GZ, ix, iy)
    for k in range(1, GY):
        greet(iz, ix, (iy + k) % GY)

    @pl.when(ix < GX - 1)
    def _():
        greet(next_first, ix + 1, iy)

    @pl.when(ix > 0)
    def _():
        greet(prev_last, ix - 1, iy)

    @pl.when(cross_left)
    def _():
        for z in range(GZ):
            greet(z, ix - 1, iy)

    @pl.when(cross_right)
    def _():
        for z in range(GZ):
            greet(z, ix + 1, iy)

    more_left, more_right = (ix + 7) // 8, 1 - ix // 7
    pl.semaphore_wait(
        barrier,
        (GZ - 1) + (GY - 1) + more_left + more_right + 8 * first * more_left + 8 * last * more_right,
    )

    def window_copies(src_rows, dst_rows, count, kind, slot, owner, target, send, recv):
        made = []
        for n, (plane_ref, window) in enumerate(((v_ref, win_v), (s_ref, win_s))):
            made.append(
                remote(
                    plane_ref.at[:, pl.ds(src_rows, count)],
                    window.at[pl.ds(2 * owner, 2), pl.ds(dst_rows, count)],
                    send.at[n, kind, slot],
                    recv.at[n, kind, owner],
                    target,
                )
            )
        return made

    def mates(action):
        for k in range(1, GZ):
            z = (iz + k) % GZ
            pz = even * z + (1 - even) * (7 - z)
            target = dev(z, ix, iy)
            action(window_copies(16 * pz, 8, 16, 0, k, iz, target, w_send, w_recv))

            @pl.when(pz > 0)
            def _():
                action(window_copies(16 * pz - 8, 0, 8, 1, k, iz, target, w_send, w_recv))

            @pl.when(pz < 7)
            def _():
                action(window_copies(16 * pz + 16, 24, 8, 2, k, iz, target, w_send, w_recv))

        @pl.when(ix < GX - 1)
        def _():
            action(window_copies(120, 0, 8, 0, 0, iz, dev(next_first, ix + 1, iy), wx_send, wx_recv))

        @pl.when(ix > 0)
        def _():
            action(window_copies(0, 24, 8, 1, 0, iz, dev(prev_last, ix - 1, iy), wx_send, wx_recv))

    def start_all(copies):
        for copy in copies:
            copy.start()

    def sent_all(copies):
        for copy in copies:
            copy.wait_send()

    def got_all(copies):
        for copy in copies:
            copy.wait_recv()

    mates(start_all)

    def a_right():
        return remote(a_ref.at[pl.ds(120, 8)], aw.at[pl.ds(0, 8)], ar_send.at[0], ar_recv.at[0], dev(iz, ix + 1, iy))

    def a_left():
        return remote(a_ref.at[pl.ds(0, 8)], aw.at[pl.ds(24, 8)], ar_send.at[1], ar_recv.at[1], dev(iz, ix - 1, iy))

    @pl.when(cross_right)
    def _():
        a_right().start()

    @pl.when(cross_left)
    def _():
        a_left().start()

    for plane_ref, window in ((v_ref, win_v), (s_ref, win_s)):
        window[pl.ds(2 * iz, 2), 8:24] = plane_ref[:, pl.ds(pl.multiple_of(16 * p, 8), 16)]

        @pl.when(p > 0)
        def _():
            window[pl.ds(2 * iz, 2), 0:8] = plane_ref[:, pl.ds(pl.multiple_of(16 * p - 8, 8), 8)]

        @pl.when(p < 7)
        def _():
            window[pl.ds(2 * iz, 2), 24:32] = plane_ref[:, pl.ds(pl.multiple_of(16 * p + 16, 8), 8)]

    for k in range(1, GZ):
        z = (iz + k) % GZ
        me = dev((iz + 1) % GZ, ix, iy)
        got_all(window_copies(0, 8, 16, 0, k, z, me, w_send, w_recv))

        @pl.when(p > 0)
        def _():
            got_all(window_copies(0, 0, 8, 1, k, z, me, w_send, w_recv))

        @pl.when(p < 7)
        def _():
            got_all(window_copies(0, 24, 8, 2, k, z, me, w_send, w_recv))

    @pl.when(cross_left)
    def _():
        for z in range(GZ):
            got_all(window_copies(0, 0, 8, 0, 0, z, dev(iz, ix - 1, iy), wx_send, wx_recv))

    @pl.when(cross_right)
    def _():
        for z in range(GZ):
            got_all(window_copies(0, 24, 8, 1, 0, z, dev(iz, ix + 1, iy), wx_send, wx_recv))

    zero_plane = jnp.zeros((128, 128), jnp.float32)
    field[0] = zero_plane
    field[NZ + 1] = zero_plane
    edge[0] = jnp.zeros((8, 128), jnp.float32)
    edge[NZ + 1] = jnp.zeros((8, 128), jnp.float32)

    def turn_plane(z, c):
        w = win_v[z]
        field[z + 1] = jnp.concatenate([w] * GROUPS, axis=0).T
        w = win_s[z]
        source[z] = jnp.concatenate([w] * GROUPS, axis=0).T
        return c

    lax.fori_loop(0, NZ, turn_plane, 0)
    for z in range(NZ):
        ve_out[2 * z : 2 * z + 1] = field[z + 1, 0:1]
        ve_out[2 * z + 1 : 2 * z + 2] = field[z + 1, 127:128]

    def to_blocks(src, dst, send, recv, k):
        return remote(src, dst.at[iy], send.at[k], recv.at[iy], dev(iz, ix, (iy + k) % GY))

    def from_blocks(src, dst, send, recv, k):
        y = (iy + k) % GY
        return remote(src, dst.at[y], send.at[k], recv.at[y], dev(iz, ix, y))

    for k in range(1, GY):
        to_blocks(ve_out, ve_in, ve_send, ve_recv, k).start()
    ve_in[iy] = ve_out[...]

    a_mid.wait()

    @pl.when(p > 0)
    def _():
        a_low().wait()

    @pl.when(p < 7)
    def _():
        a_high().wait()

    @pl.when(cross_left)
    def _():
        a_right().wait_recv()

    @pl.when(cross_right)
    def _():
        a_left().wait_recv()

    def turn_block(i_lo, c):
        parts = [aw[:, pl.ds(h * WIN + i_lo, 1), :].reshape(WIN, 128) for h in range(GROUPS)]
        a2[i_lo] = jnp.concatenate(parts, axis=0).T
        return c

    lax.fori_loop(0, WIN, turn_block, 0)

    def block_product(residual):
        out = []
        for b in range(4):
            accs = []
            for k in range(8):
                acc = a2[8 * b + k, 0:8] * residual[0:8]
                for m in range(1, 16):
                    acc = acc + a2[8 * b + k, 8 * m : 8 * m + 8] * residual[8 * m : 8 * m + 8]
                accs.append(acc)
            out.append(row_sums(accs))
        return unpack(jnp.concatenate(out, axis=0))

    def sum_y(x, low, high):
        shift[8:136] = x
        shift[7:8] = low
        shift[136:137] = high
        return shift[7:135] + x + shift[9:137]

    zero_row = jnp.zeros((1, 128), jnp.float32)

    ends = (0, 127)
    for n, end in enumerate(ends):
        cols[n] = unpack(jnp.concatenate([a2[i, end : end + 1] for i in range(WIN)], axis=0))
        row = a2[end % WIN]
        group = lane_group((128, 128))
        out = row
        for m in range(1, GROUPS):
            out = jnp.where(group == (end // WIN + m) % GROUPS, lane_roll(row, WIN * m), out)
        rows_t[n] = sum_y(out, zero_row, zero_row)
    for side in range(2):
        for n in range(2):
            first_tap = 2 * (side != n) + side
            g_out[first_tap : first_tap + 1] = cols[n, ends[side] : ends[side] + 1]

    def second(index, c):
        n, off = index // 3, index % 3 - 1
        col = cols[n]
        shifted = jnp.where(off == 0, col, jnp.where(off > 0, lane_roll(col, -1), lane_roll(col, 1)))
        cols[2 + index] = block_product(sum_y(shifted, zero_row, zero_row))
        return c

    lax.fori_loop(0, 6, second, 0)
    third = {}
    for n in range(2):
        for off in (-1, 0, 1):
            col = cols[2 + 3 * n + off + 1]
            tap = TAPS.index((2, off))
            for side in range(2):
                at = 4 * tap + 2 * (side != n) + side
                g_out[at : at + 1] = col[ends[side] : ends[side] + 1]
                row = rows_t[side]
                for step in (-1, 0, 1):
                    part = jnp.sum(lane_roll(row, step) * col, axis=0, keepdims=True)
                    part = lane_roll(jnp.broadcast_to(part, (8, 128)), -step)
                    key = (n, side, step + off)
                    third[key] = part if key not in third else third[key] + part
    for (n, side, off), part in third.items():
        at = 4 * TAPS.index((3, off)) + 2 * (side != n) + side
        g_out[at : at + 1] = part[0:1]
    g_out[36:40] = jnp.zeros((4, 128), jnp.float32)
    for k in range(1, GY):
        to_blocks(g_out, g_in, g_send, g_recv, k).start()
    g_in[iy] = g_out[...]

    for k in range(1, GY):
        from_blocks(ve_out, ve_in, ve_send, ve_recv, k).wait_recv()
    for z in range(NZ):
        for y in range(GY):
            edge[z + 1, 2 * y : 2 * y + 2] = ve_in[y, 2 * z : 2 * z + 2]

    def plane_at(rr, j):
        t = STEPS * rr + j
        forward = 1 - rr // (ROUNDS // 2)
        return forward * t + (1 - forward) * (2 * NZ - 1 - t), 2 * forward - 1

    def set_base(rr):
        def one(j, c):
            z, ahead = plane_at(rr, j)
            centre = field[z + 1]
            edges = swap_edges(edge[z + 1] + edge[z + 1 + ahead])
            inject[5] = edges
            low = inject[5, pl.ds(2 * iy, 1)]
            high = inject[5, pl.ds(2 * iy + 1, 1)]
            both = sum_y(box_x(centre + field[z + 1 + ahead]), low, high)
            base[z] = source[z] - (27.0 * centre - both)
            return c

        lax.fori_loop(0, STEPS, one, 0)

    def advance(z, slot):
        low = inject[slot, pl.ds(2 * iy, 1)]
        high = inject[slot, pl.ds(2 * iy + 1, 1)]
        residual = base[z] + sum_y(box_x(prev[...]), low, high)
        return field[z + 1] + block_product(residual)

    def x_copies(rr):
        out = []
        for side, (z, x) in enumerate(((rz, rx), (lz, lx))):
            for n, (start, count) in enumerate(((STEPS * rr + 3, 1), (STEPS * rr, 3))):
                rows = pl.ds(start, count)
                out.append(
                    remote(
                        xs.at[rows], xr.at[side, rows],
                        x_send.at[side, n, rr], x_recv.at[side, n, rr], dev(z, x, iy),
                    )
                )
        return out

    def last_copies():
        return [
            remote(xs_last, xr_last.at[side], x_send.at[side, 0, 4], x_recv.at[side, 0, 4], dev(z, x, iy))
            for side, (z, x) in enumerate(((rz, rx), (lz, lx)))
        ]

    def when_sides(make, pick, to_do, sending):
        @pl.when(has_right if sending else has_left)
        def _():
            copies = make()
            to_do([copies[n] for n in pick(len(copies), 0)])

        @pl.when(has_left if sending else has_right)
        def _():
            copies = make()
            to_do([copies[n] for n in pick(len(copies), 1)])

    def pick_all(count, side):
        return range(side * count // 2, (side + 1) * count // 2)

    def pick_first(count, side):
        return range(side * count // 2, side * count // 2 + 1)

    def pick_rest(count, side):
        return range(side * count // 2 + 1, (side + 1) * count // 2)

    def merged(own, left, right):
        x = lax.broadcasted_iota(jnp.int32, own.shape, 1) % WIN
        return jnp.where(x < HALO, lane_roll(left, -OWN), jnp.where(x >= HALO + OWN, lane_roll(right, OWN), own))

    def emit(rr):
        for pair in range(2):
            m = (2 * NZ - 1 - STEPS * rr) // 2 - pair
            for n in range(2):
                g_stage[2 * m + n] = field[2 * m + n + 1].T[HALO : HALO + OWN]

            @pl.when(m == iz)
            def _():
                out_buf[:, pl.ds(pl.multiple_of(16 * p, 8), 16)] = g_stage[pl.ds(2 * iz, 2)]

            @pl.when(m != iz)
            def _():
                out_copy(m).start()

    def out_copy(m):
        return remote(
            g_stage.at[pl.ds(2 * m, 2)],
            out_buf.at[:, pl.ds(16 * p, 16)],
            f_send.at[m],
            f_recv.at[iz],
            dev(m, ix, iy),
        )

    zero_tile = jnp.zeros((8, 128), jnp.float32)
    inject[0] = zero_tile
    inject[4] = zero_tile
    prev[...] = zero_plane
    set_base(0)

    def one_round(rr, c):
        slot = rr % 2

        def free(j, c):
            z, _ = plane_at(rr, j)
            fresh = advance(z, 4 * ((j + 3) // 4))
            prev[...] = fresh
            phi_out[slot, pl.ds(2 * j, 1)] = fresh[0:1]
            phi_out[slot, pl.ds(2 * j + 1, 1)] = fresh[127:128]

            @pl.when(j == 0)
            def _():
                field[z + 1] = fresh

            return c

        lax.fori_loop(0, STEPS, free, 0)
        for k in range(1, GY):
            to_blocks(phi_out.at[slot], phi_in.at[slot], phi_send.at[slot], phi_recv.at[slot], k).start()
        phi_in[slot, iy] = phi_out[slot]

        z0, _ = plane_at(rr, 0)
        prev[...] = field[z0 + 1]

        @pl.when((rr != ROUNDS // 2 - 1) & (rr < ROUNDS - 1))
        def _():
            set_base(rr + 1)

        @pl.when(rr > ROUNDS // 2)
        def _():
            emit(rr - 1)

        @pl.when(rr == 0)
        def _():
            for k in range(1, GY):
                from_blocks(g_out, g_in, g_send, g_recv, k).wait_recv()
            for tap in range(len(TAPS)):
                for kind in range(2):
                    for y in range(GY):
                        at = 4 * tap + 2 * kind
                        taps[tap, kind, 2 * y : 2 * y + 2] = g_in[y, at : at + 2]

        for k in range(1, GY):
            from_blocks(phi_out.at[slot], phi_in.at[slot], phi_send.at[slot], phi_recv.at[slot], k).wait()
        for j in range(STEPS):
            for y in range(GY):
                phi[j, 2 * y : 2 * y + 2] = phi_in[slot, y, 2 * j : 2 * j + 2]
        injected = []
        for j in range(STEPS):
            edges = phi[j]
            for lag in range(1, j + 1):
                straight, crossed = injected[j - lag]
                for off in range(1 - lag, lag):
                    tap = TAPS.index((lag, off))
                    edges = edges + taps[tap, 0] * lane_roll(straight, -off) + taps[tap, 1] * lane_roll(crossed, -off)
            z, _ = plane_at(rr, j)
            edge[z + 1] = edges
            straight = swap_edges(edges)
            injected.append((straight, swap_sides(straight)))
            inject[(j + 1) % STEPS] = straight

        def true(j, c):
            z, _ = plane_at(rr, j)
            fresh = advance(z, j)
            prev[...] = fresh
            field[z + 1] = fresh
            return c

        lax.fori_loop(1, STEPS, true, 0)

        @pl.when(rr < ROUNDS // 2)
        def _():
            for j in range(STEPS):
                z = STEPS * rr + j
                xs[z, 0:32] = pack(field[z + 1])
                xs[z, 32:40] = edge[z + 1]
            when_sides(lambda: x_copies(rr), pick_all, start_all, True)

        @pl.when(rr == 1)
        def _():
            when_sides(lambda: x_copies(rr), pick_first, got_all, False)
            z = 2 * STEPS - 1
            fresh = unpack(merged(xs[z, 0:32], xr[0, z, 0:32], xr[1, z, 0:32]))
            prev[...] = fresh
            inject[0] = swap_edges(merged(xs[z, 32:40], xr[0, z, 32:40], xr[1, z, 32:40]))

        @pl.when(rr == 3)
        def _():
            for r in (0, 2, 3):
                when_sides(lambda: x_copies(r), pick_first, got_all, False)
            for r in range(4):
                when_sides(lambda: x_copies(r), pick_rest, got_all, False)

            def one(z, c):
                field[z + 1] = unpack(merged(xs[z, 0:32], xr[0, z, 0:32], xr[1, z, 0:32]))
                edge[z + 1] = merged(xs[z, 32:40], xr[0, z, 32:40], xr[1, z, 32:40])
                return c

            lax.fori_loop(0, NZ, one, 0)
            prev[...] = zero_plane
            inject[0] = zero_tile
            set_base(ROUNDS // 2)

        @pl.when(rr == 5)
        def _():
            xs_last[0:32] = pack(prev[...])
            xs_last[32:40] = edge[NZ // 2 + 1]
            when_sides(last_copies, pick_all, start_all, True)
            when_sides(last_copies, pick_all, got_all, False)
            prev[...] = unpack(merged(xs_last[0:32], xr_last[0, 0:32], xr_last[1, 0:32]))
            inject[0] = swap_edges(merged(xs_last[32:40], xr_last[0, 32:40], xr_last[1, 32:40]))

        return c

    lax.fori_loop(0, ROUNDS, one_round, 0)
    emit(ROUNDS - 1)

    mates(sent_all)

    @pl.when(cross_right)
    def _():
        a_right().wait_send()

    @pl.when(cross_left)
    def _():
        a_left().wait_send()

    for k in range(1, GY):
        to_blocks(ve_out, ve_in, ve_send, ve_recv, k).wait_send()
        to_blocks(g_out, g_in, g_send, g_recv, k).wait_send()
    for r in range(4):
        when_sides(lambda: x_copies(r), pick_all, sent_all, True)
    when_sides(last_copies, pick_all, sent_all, True)
    for k in range(1, GZ):
        z = (iz + k) % GZ
        out_copy(z).wait_send()
        remote(
            g_stage.at[pl.ds(0, 2)], out_buf.at[:, pl.ds(0, 16)], f_send.at[z], f_recv.at[z], dev(z, ix, iy)
        ).wait_recv()
    o_ref[...] = out_buf[...]


def body(initial_field, source_term, block_inverse):
    f32 = jnp.float32
    dma = pltpu.SemaphoreType.DMA
    vmem = pltpu.VMEM
    return pl.pallas_call(
        kernel,
        out_shape=jax.ShapeDtypeStruct(initial_field.shape, f32),
        in_specs=[
            pl.BlockSpec(memory_space=pltpu.VMEM),
            pl.BlockSpec(memory_space=pltpu.VMEM),
            pl.BlockSpec(memory_space=pl.ANY),
        ],
        out_specs=pl.BlockSpec(memory_space=pltpu.VMEM),
        scratch_shapes=[
            vmem((WIN, 128, 128), f32),
            vmem((WIN, 128, 128), f32),
            vmem((NZ, WIN, 128), f32),
            vmem((NZ, WIN, 128), f32),
            vmem((NZ + 2, 128, 128), f32),
            vmem((NZ, 128, 128), f32),
            vmem((NZ, 128, 128), f32),
            vmem((NZ + 2, 8, 128), f32),
            vmem((128, 128), f32),
            vmem((144, 128), f32),
            vmem((6, 8, 128), f32),
            vmem((2, 8, 128), f32),
            vmem((2, GY, 8, 128), f32),
            vmem((STEPS, 8, 128), f32),
            vmem((2 * NZ, 128), f32),
            vmem((GY, 2 * NZ, 128), f32),
            vmem((TAP_ROWS, 128), f32),
            vmem((GY, TAP_ROWS, 128), f32),
            vmem((len(TAPS), 2, 8, 128), f32),
            vmem((8, 128, 128), f32),
            vmem((2, 128, 128), f32),
            vmem((NZ, 40, 128), f32),
            vmem((2, NZ, 40, 128), f32),
            vmem((40, 128), f32),
            vmem((2, 40, 128), f32),
            vmem((NZ, OWN, 128), f32),
            vmem((2, 128, 128), f32),
            dma((3,)),
            dma((2,)),
            dma((2,)),
            dma((2, 3, GZ)),
            dma((2, 3, GZ)),
            dma((2, 2, 1)),
            dma((2, 2, GZ)),
            dma((2, GY)),
            dma((2, GY)),
            dma((GY,)),
            dma((GY,)),
            dma((GY,)),
            dma((GY,)),
            dma((2, 2, 5)),
            dma((2, 2, 5)),
            dma((GZ,)),
            dma((GZ,)),
        ],
        compiler_params=pltpu.CompilerParams(collective_id=0, has_side_effects=True),
    )(initial_field, source_term, block_inverse)


def solution(mesh):
    placed = (P("gz", "gx", "gy"), P("gz", "gx", "gy"), P("gx", "gy", None))
    return jax.shard_map(
        body, mesh=mesh, in_specs=placed, out_specs=P("gz", "gx", "gy"), check_vma=False
    )
```

time: 1360 us -> 105 us (0.08)
  the two profiles are of different devices: /device:TPU:166 before, /device:TPU:7 now
where the time goes in v1:
time: 105 us
  Pallas kernels  103 us (98%)
  local copies, waits for them, and re-layouts  1.57 us (1%)
    pallas_call x1, Pallas kernels, body(): pl.pallas_call(kernel, out_shape=jax.ShapeDtypeStruct(initial_field.shape...  103 us

profile of v1, /device:TPU:7, one launch (start us, length us, event | category | flops | bytes accessed | tf_op | source)
XLA Modules:
  0.0 104.8 jit_solution(9550576931885439350)
XLA Ops:
  0.0 103.2 %shard_map.37 = f32[2,128,128]{2,1,0:T(8,128)} custom-call(f32[2,128,128]{2,1,0:T(8,128)} %v_ref.1, f32[2,128,128]{2,1,0:T(8,128)} %s_ref.1, f32[128,128,128]{2,1,0:T(8,128)} %a_ref.1), custom_call_target="tpu_custom_call" | custom-call | tf_op jit(solution)/shard_map/pallas_call | solution.py:642
  103.2 1.6 %copy.5 = f32[2,128,128]{2,1,0:T(8,128)} copy(f32[2,128,128]{2,1,0:T(8,128)} %shard_map.37) | data formatting | bytes 262144
